TPU v7x, 32 devices: a whole 2x2x4 slice. The times are simulated.
32 devices in a mesh: sec: 2 (over y), dev: 16 (over z, x, core).
Axes of the slice: x: 2, y: 2, z: 4, core: 2. Of those that a mesh axis runs over, the one named last changes fastest.
Arguments:
- flow_state: float32 [5, 8, 1024, 512], P(None, None, ('sec', 'dev')), may hold values from -6 to 6
- diffusion: float32 [8, 1024, 512], P(None, ('sec', 'dev')), may hold values from 0.02 to 0.1
- wall_stress: float32 [2, 1024, 512], P(None, ('sec', 'dev')), may hold values from -3 to 3
- batch_counts: int32 [32, 48], P(('sec', 'dev')), may hold values from 1 to 4, 120 in all within a row
- batch_routes: int32 [1536, 1], P(('sec', 'dev')), may hold values from 0 to 31; in each aligned block of 48 rows (0 to 47, 48 to 95, ...) at most 2 rows name the same one
- wall_index: int32 [1536, 4], P(('sec', 'dev')), may hold values from 0 to 16383, as said below
- input_weight: bfloat16 [12, 2048], replicated, may hold values from -1.75 to 1.75
- middle_weight: bfloat16 [2048, 2048], P(('sec', 'dev')), may hold values from -0.125 to 0.125
- output_weight: bfloat16 [2, 2048], replicated, may hold values from -0.125 to 0.125
Outputs:
- new_field: float32 [5, 8, 1024, 512], P(None, None, ('sec', 'dev'))
- new_stress: float32 [2, 1024, 512], P(None, ('sec', 'dev'))
- batch_loss: float32 [32], P(('sec', 'dev'))
- grad_w_in: float32 [12, 2048], replicated
- grad_w_mid: float32 [2048, 2048], P(('sec', 'dev'))
Inputs may be any that keep to these rules, and one draw needn't show every extreme that they name: `batch_routes`: within the 48 rows of one device no trainer is named more than 2 times, and every trainer is named by some row. `batch_counts`: each device's row sums to 120. `wall_index`: all entries of the 48 rows of one device are distinct.
All inputs are finite; a program needn't handle non-finite values.
Results may differ from a plain program's by a relative error of at most 0.00091.
Values may be sent and summed in bfloat16 or wider, within the bound.
No kernel may reach another device: no remote copies, remote signals or barrier semaphores. Data moves between devices by JAX's collectives and lax.ppermute only.
A program may use at most 128 MiB of HBM per device.

v0:
```python
import math
import jax
import jax.numpy as jnp
from jax import lax
from jax.sharding import PartitionSpec as P

SLOTS = 2
advect_number = 0.3
wall_gain = 0.5
grad_number = 32.0


def extended(block, sides, width):
    for axis, dim in sides:
        count = lax.axis_size(axis)
        forward = [(i, i + 1) for i in range(count - 1)]
        forward.append((count - 1, 0))
        backward = [(target, source) for source, target in forward]
        low = lax.ppermute(
            lax.slice_in_dim(block, block.shape[dim] - width, None, axis=dim), axis, forward
        )
        high = lax.ppermute(lax.slice_in_dim(block, 0, width, axis=dim), axis, backward)
        block = jnp.concatenate([low, block, high], axis=dim)
    return block


def advance(flow_state, diffusion, below_z, above_z):
    below_x = jnp.concatenate([flow_state[..., :1], flow_state[..., :-1]], axis=3)
    above_x = jnp.concatenate([flow_state[..., 1:], flow_state[..., -1:]], axis=3)
    below_y = jnp.concatenate([flow_state[:, :1], flow_state[:, :-1]], axis=1)
    above_y = jnp.concatenate([flow_state[:, 1:], flow_state[:, -1:]], axis=1)
    spread = below_x + above_x + below_y + above_y + below_z + above_z - 6.0 * flow_state
    return flow_state + advect_number * (below_x - flow_state) + diffusion[None] * spread


def wall_columns(flow_state):
    points = flow_state.shape[2] * flow_state.shape[3]
    inputs = flow_state[0:4, 0:3].reshape(12, points)
    targets = jnp.stack(
        [flow_state[1, 4] - flow_state[1, 3], flow_state[3, 4] - flow_state[3, 3]]
    ).reshape(2, points)
    return jnp.concatenate([inputs, targets], axis=0).astype(jnp.bfloat16)


def apply_wall(advanced, new_stress):
    advanced = advanced.at[1, 0].add(-wall_gain * new_stress[0])
    return advanced.at[3, 0].add(-wall_gain * new_stress[1])


def contract_first(left, right):
    return lax.dot_general(
        left, right, (((0,), (0,)), ((), ())), preferred_element_type=jnp.float32
    )


def contract_last(left, right):
    return lax.dot_general(
        left, right, (((1,), (1,)), ((), ())), preferred_element_type=jnp.float32
    )


def body(
    flow_state,
    diffusion,
    wall_stress,
    batch_counts,
    batch_routes,
    wall_index,
    input_weight,
    middle_weight,
    output_weight,
):
    tile_count, capacity = wall_index.shape
    devices = lax.axis_size(("sec", "dev"))
    channels = 14
    slot_total = devices * SLOTS
    row_total = slot_total * capacity
    points = flow_state.shape[2] * flow_state.shape[3]
    columns = wall_columns(flow_state)
    picked = jnp.take(columns, wall_index.reshape(-1), axis=1).reshape(
        channels, tile_count, capacity
    )
    is_live = (
        jnp.arange(capacity, dtype=jnp.int32)[None, :] < batch_counts.reshape(tile_count)[:, None]
    )
    picked = jnp.where(is_live[None], picked, jnp.zeros((), jnp.bfloat16))
    destination = batch_routes.reshape(tile_count)
    matches = (destination[:, None] == jnp.arange(devices, dtype=jnp.int32)[None, :]).astype(
        jnp.int32
    )
    slot_rank = jnp.sum((jnp.cumsum(matches, axis=0) - matches) * matches, axis=1)
    slot_id = destination * SLOTS + slot_rank
    placing = (slot_id[:, None] == jnp.arange(slot_total, dtype=jnp.int32)[None, :]).astype(
        jnp.bfloat16
    )
    send_rows = jnp.einsum(
        "bs,cbk->sck", placing, picked, preferred_element_type=jnp.float32
    ).astype(jnp.bfloat16)
    send_rows = send_rows.reshape(devices, SLOTS, channels, capacity)
    send_live = jnp.einsum(
        "bs,bk->sk", placing, is_live.astype(jnp.bfloat16), preferred_element_type=jnp.float32
    ).astype(jnp.bfloat16)
    send_live = send_live.reshape(devices, SLOTS, capacity)
    got_rows, got_live = (
        lax.all_to_all(send_rows, ("sec", "dev"), split_axis=0, concat_axis=0, tiled=True),
        lax.all_to_all(send_live, ("sec", "dev"), split_axis=0, concat_axis=0, tiled=True),
    )
    sample_rows = jnp.transpose(got_rows, (0, 1, 3, 2)).reshape(row_total, channels)
    features = sample_rows[:, :12]
    targets = sample_rows[:, 12:].astype(jnp.float32)
    live_rows = got_live.reshape(row_total).astype(jnp.float32)
    pre_first = jnp.dot(features, input_weight, preferred_element_type=jnp.float32)
    first_tanh = jnp.tanh(pre_first)
    first_act = first_tanh.astype(jnp.bfloat16)
    part = first_act
    pre_second = jnp.dot(
        part,
        lax.all_gather(middle_weight, ("sec", "dev"), axis=0, tiled=True),
        preferred_element_type=jnp.float32,
    )
    second_tanh = jnp.tanh(pre_second)
    second_act = second_tanh.astype(jnp.bfloat16)
    prediction = contract_last(second_act, output_weight)
    errors = (prediction - targets) * live_rows[:, None]
    sent_back = jnp.transpose(
        prediction.astype(jnp.bfloat16).reshape(devices, SLOTS, capacity, 2), (0, 1, 3, 2)
    )
    answers = lax.all_to_all(sent_back, ("sec", "dev"), split_axis=0, concat_axis=0, tiled=True)
    answers = answers.reshape(slot_total, 2, capacity)
    live_total = jnp.sum(live_rows)
    batch_loss = (0.5 * jnp.sum(errors * errors) / live_total).reshape(1)
    live_dev = 5 * tile_count * capacity // 8
    scale = grad_number / math.sqrt(live_dev * devices)
    back_out = (errors * scale).astype(jnp.bfloat16)
    back_second = (
        jnp.dot(back_out, output_weight, preferred_element_type=jnp.float32)
        * (1.0 - second_tanh * second_tanh)
    ).astype(jnp.bfloat16)
    back_hidden = contract_last(
        back_second, lax.all_gather(middle_weight, ("sec", "dev"), axis=0, tiled=True)
    )
    back_first = (back_hidden * (1.0 - first_tanh * first_tanh)).astype(jnp.bfloat16)
    part = first_act
    grad_w_mid = lax.psum_scatter(
        contract_first(part, back_second), ("sec", "dev"), scatter_dimension=0, tiled=True
    )
    grad_w_in = lax.psum(contract_first(features, back_first), ("sec", "dev"))
    per_tile = jnp.einsum("bs,sck->cbk", placing, answers, preferred_element_type=jnp.float32)
    target_index = jnp.where(is_live, wall_index, points).reshape(-1)
    new_stress = (
        wall_stress.reshape(2, points)
        .at[:, target_index]
        .set(per_tile.reshape(2, -1), mode="drop")
        .reshape(wall_stress.shape)
    )
    padded = extended(flow_state.astype(jnp.bfloat16), ((("sec", "dev"), 2),), 1).astype(
        flow_state.dtype
    )
    advanced = advance(flow_state, diffusion, padded[:, :, :-2], padded[:, :, 2:])
    new_field = apply_wall(advanced, new_stress)
    return (new_field, new_stress, batch_loss, grad_w_in, grad_w_mid)


def solution(mesh):
    in_specs = (
        P(None, None, ("sec", "dev"), None),
        P(None, ("sec", "dev"), None),
        P(None, ("sec", "dev"), None),
        P(("sec", "dev"), None),
        P(("sec", "dev"), None),
        P(("sec", "dev"), None),
        P(),
        P(("sec", "dev"), None),
        P(),
    )
    out_specs = (
        P(None, None, ("sec", "dev"), None),
        P(None, ("sec", "dev"), None),
        P(("sec", "dev")),
        P(),
        P(("sec", "dev"), None),
    )
    return jax.shard_map(body, mesh=mesh, in_specs=in_specs, out_specs=out_specs, check_vma=False)
```

profile of v0, /device:TPU:9, one launch (start us, length us, event | category | flops | bytes accessed | tf_op | source)
XLA Modules:
  0.0 425.7 jit_solution(3434637611886213195)
XLA Ops:
  7.2 0.7 all-gather.2.cloned.1.call-update
  7.9 0.8 fusion.25
  8.8 0.8 select_reduce_fusion
  9.6 0.7 fusion.36
  10.3 0.8 convolution_convert_fusion.1
  11.2 0.7 copy.49
  11.9 6.3 %all-to-all-start.2 = ((bf16[32,2,4]{2,1,0:T(2,128)(2,1)}), bf16[32,2,4]{2,1,0:T(2,128)(2,1)S(1)}, u32[]{:S(2)}, u32[]{:S(2)}) async-start(bf16[32,2,4]{2,1,0:T(2,128)(2,1)} %bitcast.18), calls=%async_computation.2 | async-start | bytes 32768 | tf_op jit(solution)/shard_map/all_to_all | solution.py:106
  18.2 0.8 copy.37
  19.1 2.0 convert_element_type.52
  21.3 1.0 copy-done.3
  22.3 0.3 copy.53
  22.6 0.2 pad_maximum_fusion.1
  22.9 3.4 copy.38
  26.3 3.4 gather_fusion
  29.8 0.2 convolution_convert_fusion
  30.0 0.1 copy.40
  30.2 0.7 copy.41
  30.8 5.8 %all-to-all-start = ((bf16[32,2,14,4]{2,1,3,0:T(2,128)(2,1)}), bf16[32,2,14,4]{2,1,3,0:T(2,128)(2,1)S(1)}, u32[]{:S(2)}, u32[]{:S(2)}) async-start(bf16[32,2,14,4]{2,1,3,0:T(2,128)(2,1)} %copy.41), calls=%async_computation | async-start | bytes 131072 | tf_op jit(solution)/shard_map/all_to_all | solution.py:105
  36.9 5.8 %all-to-all-done = bf16[32,2,14,4]{2,1,3,0:T(2,128)(2,1)S(1)} async-done(((bf16[32,2,14,4]{2,1,3,0:T(2,128)(2,1)}), bf16[32,2,14,4]{2,1,3,0:T(2,128)(2,1)S(1)}, u32[]{:S(2)}, u32[]{:S(2)}) %all-to-all-start) | async-done | bytes 7200 | tf_op jit(solution)/shard_map/all_to_all | solution.py:105
  42.9 1.8 convolution_tanh_fusion.1
  44.6 44.9 %all-gather.2.cloned.1.call-done = bf16[2048,2048]{1,0:T(8,128)(2,1)} async-done(((bf16[64,2048]{1,0:T(8,128)(2,1)}), bf16[2048,2048]{1,0:T(8,128)(2,1)}) %all-gather.2.cloned.1.call-update) | async-done | bytes 8388624 | tf_op jit(solution)/shard_map/all_gather | solution.py:118
  89.6 6.4 %convolution_tanh_fusion = f32[256,2048]{1,0:T(8,128)S(1)} fusion(bf16[2048,2048]{1,0:T(8,128)(2,1)} %all-gather.2.cloned.1.call-done, f32[256,2048]{1,0:T(8,128)} %convolution_tanh_fusion.1), kind=kOutput, calls=%fused_computation.8 | convolution fusion | flops 2148007936 | bytes 12582912 | tf_op jit(solution)/shard_map/dot_general | solution.py:116
  96.0 1.0 multiply_reduce_fusion
  97.0 1.5 fusion.8
  98.4 7.4 %fusion.9 = f32[12,2048]{1,0:T(8,128)} fusion(bf16[256,2048]{1,0:T(8,128)(2,1)} %fusion.8, bf16[2048,2048]{1,0:T(8,128)(2,1)} %all-gather.2.cloned.1.call-done, f32[256,2048]{1,0:T(8,128)} %convolution_tanh_fusion.1, bf16[256,14]{1,0:T(8,128)(2,1)S(1)} %bitcast.59), kind=kOutput, calls=%fused_computation.22 | convolution fusion | flops 2162163712 | bytes 11639808 | tf_op jit(solution)/shard_map/dot_general | solution.py:51
  105.9 10.0 %fusion.13 = f32[2048,2048]{1,0:T(8,128)} fusion(bf16[256,2048]{1,0:T(8,128)(2,1)} %fusion.8, f32[256,2048]{1,0:T(8,128)} %convolution_tanh_fusion.1), kind=kOutput, calls=%fused_computation.30 | convolution fusion | flops 2148007936 | bytes 19922944 | tf_op jit(solution)/shard_map/dot_general | solution.py:51
  115.9 1.3 fusion.45
  117.2 1.3 collective-permute-start
  118.7 4.6 %copy.35 = f32[2,32,512]{0,2,1:T(8,128)} copy(f32[2,32,512]{2,1,0:T(8,128)S(1)} %copy-done.5) | data formatting | bytes 262144 | tf_op args[2]
  123.4 0.9 fusion.44
  124.3 1.1 fusion.41
  125.4 2.8 fusion.43
  128.2 3.4 fusion.42
  131.7 0.6 convert_reduce_fusion
  132.3 3.4 maximum_convert_fusion
  135.8 0.6 copy.43
  136.4 6.6 %all-to-all-start.1 = ((bf16[32,2,2,4]{3,1,2,0:T(2,128)(2,1)}), bf16[32,2,2,4]{3,1,2,0:T(2,128)(2,1)S(1)}, u32[]{:S(2)}, u32[]{:S(2)}) async-start(bf16[32,2,2,4]{3,1,2,0:T(2,128)(2,1)} %copy.43), calls=%async_computation.1 | async-start | bytes 65536 | tf_op jit(solution)/shard_map/all_to_all | solution.py:128
  143.1 9.2 %fusion.4 = f32[5,8,32,512]{3,2,1,0:T(8,128)} fusion(f32[5,8,34,512]{3,2,1,0:T(8,128)} %maximum_convert_fusion, f32[5,8,32,1]{3,2,1,0:T(8,128)} %get-tuple-element.49, f32[5,8,32,511]{3,2,1,0:T(8,128)} %get-tuple-element.51, f32[5,7,32,512]{3,2,1,0:T(8,128)} %get-tuple-element.53, f32[5,1,32,512]{3,2,1,0:T(8,128)} %get-tuple-element.55, ...), kind=kLoop, calls=%fused_computation.13 | loop fusion | flops 10485760 | bytes 21495808 | tf_op jit(solution)/shard_map/add | solution.py:33
  153.7 0.2 convolution_bitcast_fusion
  154.1 0.1 copy.47
  154.2 7.6 %scatter_fusion = f32[2,16384]{0,1:T(8,128)} fusion(f32[2,16384]{0,1:T(8,128)} %bitcast.52, s32[192]{0:T(256)S(1)} %bitcast.68, f32[192,2]{1,0:T(8,128)S(1)} %copy.47), kind=kCustom, calls=%fused_computation.1 | custom fusion | bytes 5376 | tf_op jit(solution)/shard_map/scatter | solution.py:153
  161.8 5.9 %copy.50 = f32[2,32,512]{2,1,0:T(8,128)} copy(f32[2,32,512]{0,2,1:T(8,128)} %bitcast.53) | data formatting | bytes 262144
  167.7 12.3 %fusion = (f32[16384]{0:T(1024)S(1)}, f32[16384]{0:T(1024)S(1)}) fusion(f32[2,16384]{0,1:T(8,128)} %scatter_fusion), kind=kLoop, calls=%fused_computation.3 | loop fusion | flops 32768 | bytes 262144 | tf_op jit(solution)/shard_map/mul | solution.py:47
  180.0 1.5 fusion.17
  181.5 1.5 fusion.16
  183.0 43.7 %all-reduce.2.cloned.1.call-done = f32[12,2048]{1,0:T(8,128)} async-done(((f32[12,2048]{1,0:T(8,128)}), f32[12,2048]{1,0:T(8,128)}) %all-reduce.2.cloned.1.call-update) | async-done | bytes 98320 | tf_op jit(solution)/shard_map/psum | solution.py:147
  226.7 189.8 %reduce-scatter.2.cloned.1.call-done = f32[64,2048]{1,0:T(8,128)} async-done(((f32[2048,2048]{1,0:T(8,128)}), f32[64,2048]{1,0:T(8,128)}) %reduce-scatter.2.cloned.1.call-update) | async-done | bytes 524304 | tf_op jit(solution)/shard_map/reduce_scatter | solution.py:144
  416.5 1.6 copy.60
  (52 shorter events, 1.6 us)
Async XLA Ops:
  7.2 35.7 %copy-start = (bf16[12,2048]{1,0:T(8,128)(2,1)S(1)}, bf16[12,2048]{1,0:T(8,128)(2,1)}, u32[]{:S(2)}) copy-start(bf16[12,2048]{1,0:T(8,128)(2,1)} %param.19) | copy-start | bytes 147460
  7.2 13.9 %copy-start.2 = (f32[5,8,32,512]{3,2,1,0:T(8,128)S(1)}, f32[5,8,32,512]{3,2,1,0:T(8,128)}, u32[]{:S(2)}) copy-start(f32[5,8,32,512]{3,2,1,0:T(8,128)} %param.13) | copy-start | bytes 7864324
  7.2 82.4 %all-gather.2.cloned.1.call-start = ((), (), s32[]{:S(2)}) async-start(), calls=%async_computation.4 | async-start | bytes 8650752 | tf_op jit(solution)/shard_map/all_gather | solution.py:118
  11.9 19.0 %all-to-all-start.2 = ((bf16[32,2,4]{2,1,0:T(2,128)(2,1)}), bf16[32,2,4]{2,1,0:T(2,128)(2,1)S(1)}, u32[]{:S(2)}, u32[]{:S(2)}) async-start(bf16[32,2,4]{2,1,0:T(2,128)(2,1)} %bitcast.18), calls=%async_computation.2 | async-start | bytes 32768 | tf_op jit(solution)/shard_map/all_to_all | solution.py:106
  21.1 1.2 copy-start.3
  22.9 6.9 %copy-start.7 = (s32[48,4]{0,1:T(4,128)S(1)}, s32[48,4]{0,1:T(4,128)}, u32[]{:S(2)}) copy-start(s32[48,4]{0,1:T(4,128)} %param.18) | copy-start | bytes 2308
  22.9 6.9 %copy-start.8 = (s32[1,48]{1,0:T(1,128)S(1)}, s32[1,48]{1,0:T(1,128)}, u32[]{:S(2)}) copy-start(s32[1,48]{1,0:T(1,128)} %param.16) | copy-start | bytes 580
  30.8 11.8 %all-to-all-start = ((bf16[32,2,14,4]{2,1,3,0:T(2,128)(2,1)}), bf16[32,2,14,4]{2,1,3,0:T(2,128)(2,1)S(1)}, u32[]{:S(2)}, u32[]{:S(2)}) async-start(bf16[32,2,14,4]{2,1,3,0:T(2,128)(2,1)} %copy.41), calls=%async_computation | async-start | bytes 131072 | tf_op jit(solution)/shard_map/all_to_all | solution.py:105
  36.7 190.0 %all-reduce.2.cloned.1.call-start = ((), (), s32[]{:S(2)}) async-start(), calls=%async_computation.5 | async-start | bytes 262144 | tf_op jit(solution)/shard_map/psum | solution.py:147
  44.6 51.3 %copy-start.6 = (bf16[2,2048]{1,0:T(2,128)(2,1)S(1)}, bf16[2,2048]{1,0:T(2,128)(2,1)}, u32[]{:S(2)}) copy-start(bf16[2,2048]{1,0:T(2,128)(2,1)} %param.21) | copy-start | bytes 24580
  105.9 310.7 %reduce-scatter.2.cloned.1.call-start = ((), (), s32[]{:S(2)}) async-start(), calls=%async_computation.6 | async-start | bytes 17301504 | tf_op jit(solution)/shard_map/reduce_scatter | solution.py:144
  115.9 2.8 copy-start.5
  117.2 15.1 %collective-permute-start = (bf16[5,8,1,512]{3,2,1,0:T(2,128)(2,1)S(1)}, bf16[5,8,1,512]{3,2,1,0:T(2,128)(2,1)}, u32[]{:S(2)}, u32[]{:S(2)}) collective-permute-start(bf16[5,8,1,512]{3,2,1,0:T(2,128)(2,1)S(1)} %get-tuple-element.56), channel_id=1, source_target_pairs={{0,1},{1,2},{2,3},{3,4},{4,5},{5,6},{6,7},{7,8},{8,9},{9,10},{10,1... | collective-permute-start | bytes 122888 | tf_op jit(solution)/shard_map/ppermute | solution.py:19
  118.5 13.8 %collective-permute-start.1 = (bf16[5,8,1,512]{3,2,1,0:T(2,128)(2,1)S(1)}, bf16[5,8,1,512]{3,2,1,0:T(2,128)(2,1)}, u32[]{:S(2)}, u32[]{:S(2)}) collective-permute-start(bf16[5,8,1,512]{3,2,1,0:T(2,128)(2,1)S(1)} %get-tuple-element.57), channel_id=1, source_target_pairs={{1,0},{2,1},{3,2},{4,3},{5,4},{6,5},{7,6},{8,7},{9,8},{10,9},{11,1... | collective-permute-start | bytes 122888 | tf_op jit(solution)/shard_map/ppermute | solution.py:22
  128.2 4.1 copy-start.4
  136.4 17.2 %all-to-all-start.1 = ((bf16[32,2,2,4]{3,1,2,0:T(2,128)(2,1)}), bf16[32,2,2,4]{3,1,2,0:T(2,128)(2,1)S(1)}, u32[]{:S(2)}, u32[]{:S(2)}) async-start(bf16[32,2,2,4]{3,1,2,0:T(2,128)(2,1)} %copy.43), calls=%async_computation.1 | async-start | bytes 65536 | tf_op jit(solution)/shard_map/all_to_all | solution.py:128
  167.7 250.4 %copy-start.1 = (bf16[12,2048]{1,0:T(8,128)(2,1)S(1)}, bf16[12,2048]{1,0:T(8,128)(2,1)}, u32[]{:S(2)}) copy-start(bf16[12,2048]{1,0:T(8,128)(2,1)} %param.19) | copy-start | bytes 147460
Sparse Core Ops, SparseCore 0:
  10.8 78.7 all-gather.1
  106.0 120.6 all-reduce.1
  229.6 186.8 reduce-scatter.1
where the time goes:
time: 426 us
  waiting for transfers between devices  285 us (67%)
  local copies, waits for them, and re-layouts  41.6 us (10%)
  other arithmetic  33.1 us (8%)
  matrix products  29.2 us (7%)
  starting transfers between devices  20.3 us (5%)
  between operations  16.5 us (4%)
    reduce_scatter x1, waiting for transfers between devices, body(): lax.psum_scatter(contract_first(part, back_second), ('sec', 'dev'), scatt...  190 us
    all_gather x1, waiting for transfers between devices, body(): lax.all_gather(middle_weight, ('sec', 'dev'), axis=0, tiled=True)  44.9 us
    psum x1, waiting for transfers between devices, body(): grad_w_in = lax.psum(contract_first(features, back_first), ('sec', 'dev'))  43.7 us
    dot_general x2, matrix products, contract_first(): lax.dot_general(left, right, (((0,), (0,)), ((), ())), preferred_element_...  17.4 us
    unnamed x27, local copies, waits for them, and re-layouts  14.4 us
    mul x1, other arithmetic, apply_wall(): return advanced.at[3, 0].add(-wall_gain * new_stress[1])  12.3 us
    add x1, other arithmetic, advance(): flow_state + advect_number * (below_x - flow_state)  9.22 us
  transfers between devices with their start and end apart: 8, of which 4 were waited for; matrix products, arithmetic and copies ran while one was open for 20% of the time, Pallas kernels for 0%

commit v1 on v0

--- a/solution.py
+++ b/solution.py
@@ -8,6 +8,18 @@
 advect_number = 0.3
 wall_gain = 0.5
 grad_number = 32.0
+
+
+def collect(value, axis, dim):
+    ways, here, turn = (lax.axis_size(axis), lax.axis_index(axis), value.shape[dim])
+    line, have = (value, 1)
+    while have < ways:
+        line = jnp.concatenate(
+            [line, lax.ppermute(line, axis, [(d, (d - have) % ways) for d in range(ways)])],
+            axis=dim,
+        )
+        have = 2 * have
+    return jnp.roll(line, here * turn, axis=dim)
 
 
 def extended(block, sides, width):
@@ -114,9 +126,7 @@
     first_act = first_tanh.astype(jnp.bfloat16)
     part = first_act
     pre_second = jnp.dot(
-        part,
-        lax.all_gather(middle_weight, ("sec", "dev"), axis=0, tiled=True),
-        preferred_element_type=jnp.float32,
+        part, collect(middle_weight, ("sec", "dev"), 0), preferred_element_type=jnp.float32
     )
     second_tanh = jnp.tanh(pre_second)
     second_act = second_tanh.astype(jnp.bfloat16)

time: 426 us -> 653 us (1.53)
  waiting for transfers between devices: 285 us -> 461 us
  local copies, waits for them, and re-layouts: 41.6 us -> 70.4 us
  starting transfers between devices: 20.3 us -> 42.5 us
    ppermute x0 -> x5, waiting for transfers between devices: none -> 159 us  [collect(): lax.ppermute(line, axis, [(d, (d - have) % ways) for d in range(ways)])]
    all_to_all x1, waiting for transfers between devices: 0.01 us -> 64.7 us  [body(): lax.all_to_all(send_live, ('sec', 'dev'), split_axis=0, concat_axis=0, ti...]
    all_gather x1, waiting for transfers between devices: 44.9 us -> 0.01 us  [body(): lax.all_gather(middle_weight, ('sec', 'dev'), axis=0, tiled=True)]
    unnamed x27 -> x69, local copies, waits for them, and re-layouts: 14.4 us -> 31.3 us
    ppermute x0 -> x5, starting transfers between devices: none -> 12 us  [collect(): lax.ppermute(line, axis, [(d, (d - have) % ways) for d in range(ways)])]
    concatenate x0 -> x2, local copies, waits for them, and re-layouts: none -> 7.28 us  [the longest x1 4.7 us: collect(): return jnp.roll(line, here * turn, axis=dim)]
  transfers between devices with their start and end apart: 8 -> 13, of which waited for: 4 -> 8; matrix products, arithmetic and copies ran while one was open for 20% -> 19% of each run, Pallas kernels for 0% -> 0%
where the time goes in v1:
time: 653 us; the launch traced here: 652 us
  waiting for transfers between devices  461 us (71%)
  local copies, waits for them, and re-layouts  70.4 us (11%)
  starting transfers between devices  42.5 us (7%)
  other arithmetic  33.6 us (5%)
  matrix products  28 us (4%)
  between operations  16.6 us (3%)
    reduce_scatter x1, waiting for transfers between devices, body(): lax.psum_scatter(contract_first(part, back_second), ('sec', 'dev'), scatt...  190 us
    ppermute x5, waiting for transfers between devices, collect(): lax.ppermute(line, axis, [(d, (d - have) % ways) for d in range(ways)])  159 us
    all_to_all x1, waiting for transfers between devices, body(): lax.all_to_all(send_live, ('sec', 'dev'), split_axis=0, concat_axis=0, ti...  64.7 us
    psum x1, waiting for transfers between devices, body(): grad_w_in = lax.psum(contract_first(features, back_first), ('sec', 'dev'))  41.7 us
    unnamed x69, local copies, waits for them, and re-layouts  31.3 us
    dot_general x2, matrix products, contract_first(): lax.dot_general(left, right, (((0,), (0,)), ((), ())), preferred_element_...  17.4 us
  transfers between devices with their start and end apart: 13, of which 8 were waited for; matrix products, arithmetic and copies ran while one was open for 19% of the time, Pallas kernels for 0%

profile of v1, /device:TPU:9, one launch (start us, length us, event | category | flops | bytes accessed | tf_op | source)
XLA Modules:
  0.0 651.9 jit_solution(13470376155071554720)
XLA Ops:
  8.7 5.4 collective-permute-done.2
  14.0 1.1 pad_maximum_fusion.4
  15.1 2.0 collective-permute-start.3
  17.1 14.7 %collective-permute-done.3 = bf16[128,2048]{1,0:T(8,128)(2,1)S(1)} collective-permute-done((bf16[128,2048]{1,0:T(8,128)(2,1)S(1)}, bf16[128,2048]{1,0:T(8,128)(2,1)S(1)}, u32[]{:S(2)}, u32[]{:S(2)}) %collective-permute-start.3) | collective-permute-done | bytes 524320 | tf_op jit(solution)/shard_map/ppermute | solution.py:18
  31.9 1.0 pad_maximum_fusion.2
  32.9 5.6 collective-permute-start.4
  38.5 21.2 %collective-permute-done.4 = bf16[256,2048]{1,0:T(8,128)(2,1)S(1)} collective-permute-done((bf16[256,2048]{1,0:T(8,128)(2,1)S(1)}, bf16[256,2048]{1,0:T(8,128)(2,1)S(1)}, u32[]{:S(2)}, u32[]{:S(2)}) %collective-permute-start.4) | collective-permute-done | bytes 1048608 | tf_op jit(solution)/shard_map/ppermute | solution.py:18
  59.9 3.4 collective-permute-start.5
  65.1 1.1 constant_dynamic-update-slice_fusion.2
  66.2 1.6 constant_dynamic-update-slice_fusion.1
  67.8 117.3 %collective-permute-done.5 = bf16[512,2048]{1,0:T(8,128)(2,1)S(1)} collective-permute-done((bf16[512,2048]{1,0:T(8,128)(2,1)S(1)}, bf16[512,2048]{1,0:T(8,128)(2,1)S(1)}, u32[]{:S(2)}, u32[]{:S(2)}) %collective-permute-start.5) | collective-permute-done | bytes 2097184 | tf_op jit(solution)/shard_map/ppermute | solution.py:18
  185.1 2.6 constant_dynamic-update-slice_fusion
  189.6 10.6 %all-to-all-start.2 = ((bf16[32,2,4]{2,1,0:T(2,128)(2,1)}), bf16[32,2,4]{2,1,0:T(2,128)(2,1)S(1)}, u32[]{:S(2)}, u32[]{:S(2)}) async-start(bf16[32,2,4]{2,1,0:T(2,128)(2,1)} %bitcast.18), calls=%async_computation.2 | async-start | bytes 32768 | tf_op jit(solution)/shard_map/all_to_all | solution.py:118
  200.5 1.0 copy-done.9
  202.1 1.0 pad_maximum_fusion.3
  203.1 4.6 copy.38
  208.7 3.4 gather_fusion
  213.5 1.5 convolution_convert_fusion
  216.6 64.7 %all-to-all-done.2 = bf16[32,2,4]{2,1,0:T(2,128)(2,1)S(1)} async-done(((bf16[32,2,4]{2,1,0:T(2,128)(2,1)}), bf16[32,2,4]{2,1,0:T(2,128)(2,1)S(1)}, u32[]{:S(2)}, u32[]{:S(2)}) %all-to-all-start.2) | async-done | bytes 544 | tf_op jit(solution)/shard_map/all_to_all | solution.py:118
  281.2 10.3 %all-to-all-start = ((bf16[32,2,14,4]{2,1,3,0:T(2,128)(2,1)}), bf16[32,2,14,4]{2,1,3,0:T(2,128)(2,1)S(1)}, u32[]{:S(2)}, u32[]{:S(2)}) async-start(bf16[32,2,14,4]{2,1,3,0:T(2,128)(2,1)} %copy.41), calls=%async_computation | async-start | bytes 131072 | tf_op jit(solution)/shard_map/all_to_all | solution.py:117
  292.3 5.2 all-to-all-done
  299.7 1.5 copy.52
  301.6 5.6 constant_dynamic-update-slice_fusion.11
  309.5 1.1 constant_dynamic-update-slice_fusion.7
  310.6 1.5 constant_dynamic-update-slice_fusion.6
  312.1 4.7 constant_dynamic-update-slice_fusion.5
  316.8 5.8 fusion.4
  322.6 1.0 multiply_reduce_fusion
  323.6 1.5 multiply_convert_fusion
  325.1 7.4 %fusion.13 = f32[12,2048]{1,0:T(8,128)} fusion(bf16[256,2048]{1,0:T(8,128)(2,1)} %multiply_convert_fusion, bf16[2048,2048]{1,0:T(8,128)(2,1)} %all-gather.2.cloned.1.call-done, f32[256,2048]{1,0:T(8,128)} %copy-done.8, bf16[256,14]{1,0:T(8,128)(2,1)S(1)} %bitcast.57), kind=kOutput, calls=%fused_computation.24 | convolution fusion | flops 2162163712 | bytes 11639808 | tf_op jit(solution)/shard_map/dot_general | solution.py:63
  332.8 10.0 %fusion.17 = f32[2048,2048]{1,0:T(8,128)} fusion(bf16[256,2048]{1,0:T(8,128)(2,1)} %multiply_convert_fusion, f32[256,2048]{1,0:T(8,128)} %copy-done.8), kind=kOutput, calls=%fused_computation.34 | convolution fusion | flops 2148007936 | bytes 19922944 | tf_op jit(solution)/shard_map/dot_general | solution.py:63
  342.8 1.3 fusion.51
  344.1 1.0 collective-permute-start
  345.1 4.7 copy.35
  350.7 1.1 fusion.47
  351.8 2.8 fusion.49
  354.6 3.4 fusion.48
  358.7 3.3 maximum_convert_fusion
  362.7 8.3 %all-to-all-start.1 = ((bf16[32,2,2,4]{3,1,2,0:T(2,128)(2,1)}), bf16[32,2,2,4]{3,1,2,0:T(2,128)(2,1)S(1)}, u32[]{:S(2)}, u32[]{:S(2)}) async-start(bf16[32,2,2,4]{3,1,2,0:T(2,128)(2,1)} %copy.43), calls=%async_computation.1 | async-start | bytes 65536 | tf_op jit(solution)/shard_map/all_to_all | solution.py:138
  371.0 9.2 %fusion.9 = f32[5,8,32,512]{3,2,1,0:T(8,128)} fusion(f32[5,8,34,512]{3,2,1,0:T(8,128)} %maximum_convert_fusion, f32[5,8,32,1]{3,2,1,0:T(8,128)} %get-tuple-element.49, f32[5,8,32,511]{3,2,1,0:T(8,128)} %get-tuple-element.51, f32[5,7,32,512]{3,2,1,0:T(8,128)} %get-tuple-element.53, f32[5,1,32,512]{3,2,1,0:T(8,128)} %get-tuple-element.55, ...), kind=kLoop, calls=%fused_computation.14 | loop fusion | flops 10485760 | bytes 21495808 | tf_op jit(solution)/shard_map/add | solution.py:45
  382.2 7.7 %scatter_fusion = f32[2,16384]{0,1:T(8,128)} fusion(f32[2,16384]{0,1:T(8,128)} %bitcast.50, s32[192]{0:T(256)S(1)} %bitcast.66, f32[192,2]{1,0:T(8,128)S(1)} %copy.47), kind=kCustom, calls=%fused_computation.1 | custom fusion | bytes 5376 | tf_op jit(solution)/shard_map/scatter | solution.py:163
  389.8 12.4 %fusion = (f32[16384]{0:T(1024)S(1)}, f32[16384]{0:T(1024)S(1)}) fusion(f32[2,16384]{0,1:T(8,128)} %scatter_fusion), kind=kLoop, calls=%fused_computation.3 | loop fusion | flops 32768 | bytes 262144 | tf_op jit(solution)/shard_map/mul | solution.py:59
  402.3 5.9 copy.50
  408.2 1.5 fusion.21
  409.7 1.5 fusion.20
  411.2 41.7 %all-reduce.2.cloned.1.call-done = f32[12,2048]{1,0:T(8,128)} async-done(((f32[12,2048]{1,0:T(8,128)}), f32[12,2048]{1,0:T(8,128)}) %all-reduce.2.cloned.1.call-update) | async-done | bytes 98320 | tf_op jit(solution)/shard_map/psum | solution.py:157
  452.8 189.8 %reduce-scatter.2.cloned.1.call-done = f32[64,2048]{1,0:T(8,128)} async-done(((f32[2048,2048]{1,0:T(8,128)}), f32[64,2048]{1,0:T(8,128)}) %reduce-scatter.2.cloned.1.call-update) | async-done | bytes 524304 | tf_op jit(solution)/shard_map/reduce_scatter | solution.py:154
  642.6 1.6 copy.75
  (108 shorter events, 18.7 us)
Async XLA Ops:
  7.2 294.0 %copy-start = (bf16[12,2048]{1,0:T(8,128)(2,1)S(1)}, bf16[12,2048]{1,0:T(8,128)(2,1)}, u32[]{:S(2)}) copy-start(bf16[12,2048]{1,0:T(8,128)(2,1)} %param.19) | copy-start | bytes 147460
  7.2 52.5 %copy-start.5 = (bf16[64,2048]{1,0:T(8,128)(2,1)S(1)}, bf16[64,2048]{1,0:T(8,128)(2,1)}, u32[]{:S(2)}) copy-start(bf16[64,2048]{1,0:T(8,128)(2,1)} %param.20) | copy-start | bytes 786436
  7.2 317.9 %all-gather.2.cloned.1.call-start = ((), (), s32[]{:S(2)}) async-start(), calls=%async_computation.4 | async-start | bytes 8650752 | tf_op jit(solution)/shard_map/all_gather | solution.py:150
  7.9 6.1 collective-permute-start.2
  14.0 50.2 %copy-start.11 = (bf16[64,2048]{1,0:T(8,128)(2,1)}, bf16[64,2048]{1,0:T(8,128)(2,1)S(1)}, u32[]{:S(2)}) copy-start(bf16[64,2048]{1,0:T(8,128)(2,1)S(1)} %collective-permute-done.2) | copy-start | bytes 786436
  15.1 16.8 %collective-permute-start.3 = (bf16[128,2048]{1,0:T(8,128)(2,1)S(1)}, bf16[128,2048]{1,0:T(8,128)(2,1)S(1)}, u32[]{:S(2)}, u32[]{:S(2)}) collective-permute-start(bf16[128,2048]{1,0:T(8,128)(2,1)S(1)} %pad_maximum_fusion.4), channel_id=1, source_target_pairs={{0,30},{1,31},{2,0},{3,1},{4,2},{5,3},{6,4},{7,5},{8,6},{9,7},{10,... | collective-permute-start | bytes 1572872 | tf_op jit(solution)/shard_map/ppermute | solution.py:18
  32.9 26.8 %collective-permute-start.4 = (bf16[256,2048]{1,0:T(8,128)(2,1)S(1)}, bf16[256,2048]{1,0:T(8,128)(2,1)S(1)}, u32[]{:S(2)}, u32[]{:S(2)}) collective-permute-start(bf16[256,2048]{1,0:T(8,128)(2,1)S(1)} %pad_maximum_fusion.2), channel_id=1, source_target_pairs={{0,28},{1,29},{2,30},{3,31},{4,0},{5,1},{6,2},{7,3},{8,4},{9,5},{1... | collective-permute-start | bytes 3145736 | tf_op jit(solution)/shard_map/ppermute | solution.py:18
  59.7 6.5 copy-start.3
  59.9 125.3 %collective-permute-start.5 = (bf16[512,2048]{1,0:T(8,128)(2,1)S(1)}, bf16[512,2048]{1,0:T(8,128)(2,1)S(1)}, u32[]{:S(2)}, u32[]{:S(2)}) collective-permute-start(bf16[512,2048]{1,0:T(8,128)(2,1)S(1)} %pad_maximum_fusion.1), channel_id=1, source_target_pairs={{0,24},{1,25},{2,26},{3,27},{4,28},{5,29},{6,30},{7,31},{8,0},{9,1... | collective-permute-start | bytes 6291464 | tf_op jit(solution)/shard_map/ppermute | solution.py:18
  185.1 3.0 copy-start.6
  185.1 3.2 copy-start.20
  185.1 3.6 copy-start.21
  185.1 15.1 %copy-start.2 = (f32[5,8,32,512]{3,2,1,0:T(8,128)S(1)}, f32[5,8,32,512]{3,2,1,0:T(8,128)}, u32[]{:S(2)}) copy-start(f32[5,8,32,512]{3,2,1,0:T(8,128)} %param.13) | copy-start | bytes 7864324
  188.1 113.5 %collective-permute-start.6 = (bf16[1024,2048]{1,0:T(8,128)(2,1)}, bf16[1024,2048]{1,0:T(8,128)(2,1)}, u32[]{:S(2)}, u32[]{:S(2)}) collective-permute-start(bf16[1024,2048]{1,0:T(8,128)(2,1)} %get-tuple-element.56), channel_id=1, source_target_pairs={{0,16},{1,17},{2,18},{3,19},{4,20},{5,21},{6,22},{7,23},{8,24},{9,... | collective-permute-start | bytes 12582920 | tf_op jit(solution)/shard_map/ppermute | solution.py:18
  188.7 12.9 %copy-start.23 = (s32[48]{0:T(128)}, s32[48]{0:T(128)S(1)}, u32[]{:S(2)}) copy-start(s32[48]{0:T(128)S(1)} %fusion.42) | copy-start | bytes 580
  189.6 91.6 %all-to-all-start.2 = ((bf16[32,2,4]{2,1,0:T(2,128)(2,1)}), bf16[32,2,4]{2,1,0:T(2,128)(2,1)S(1)}, u32[]{:S(2)}, u32[]{:S(2)}) async-start(bf16[32,2,4]{2,1,0:T(2,128)(2,1)} %bitcast.18), calls=%async_computation.2 | async-start | bytes 32768 | tf_op jit(solution)/shard_map/all_to_all | solution.py:118
  200.5 1.1 copy-start.9
  203.1 4.6 copy-start.16
  203.1 4.7 copy-start.22
  281.2 16.3 %all-to-all-start = ((bf16[32,2,14,4]{2,1,3,0:T(2,128)(2,1)}), bf16[32,2,14,4]{2,1,3,0:T(2,128)(2,1)S(1)}, u32[]{:S(2)}, u32[]{:S(2)}) async-start(bf16[32,2,14,4]{2,1,3,0:T(2,128)(2,1)} %copy.41), calls=%async_computation | async-start | bytes 131072 | tf_op jit(solution)/shard_map/all_to_all | solution.py:117
  291.5 161.3 %all-reduce.2.cloned.1.call-start = ((), (), s32[]{:S(2)}) async-start(), calls=%async_computation.5 | async-start | bytes 262144 | tf_op jit(solution)/shard_map/psum | solution.py:157
  297.5 0.6 copy-start.13
  301.6 15.2 %copy-start.8 = (f32[256,2048]{1,0:T(8,128)}, f32[256,2048]{1,0:T(8,128)S(1)}, u32[]{:S(2)}) copy-start(f32[256,2048]{1,0:T(8,128)S(1)} %convolution_tanh_fusion) | copy-start | bytes 6291460
  301.6 6.3 copy-start.12
  307.2 2.3 copy-start.4
  307.2 3.4 copy-start.7
  316.8 5.8 copy-start.15
  316.8 5.8 copy-start.17
  316.8 5.8 copy-start.18
  332.5 310.1 %reduce-scatter.2.cloned.1.call-start = ((), (), s32[]{:S(2)}) async-start(), calls=%async_computation.6 | async-start | bytes 17301504 | tf_op jit(solution)/shard_map/reduce_scatter | solution.py:154
  342.8 2.3 copy-start.14
  344.1 14.6 %collective-permute-start = (bf16[5,8,1,512]{3,2,1,0:T(2,128)(2,1)S(1)}, bf16[5,8,1,512]{3,2,1,0:T(2,128)(2,1)}, u32[]{:S(2)}, u32[]{:S(2)}) collective-permute-start(bf16[5,8,1,512]{3,2,1,0:T(2,128)(2,1)S(1)} %get-tuple-element.58), channel_id=1, source_target_pairs={{0,1},{1,2},{2,3},{3,4},{4,5},{5,6},{6,7},{7,8},{8,9},{9,10},{10,1... | collective-permute-start | bytes 122888 | tf_op jit(solution)/shard_map/ppermute | solution.py:31
  345.1 13.6 %collective-permute-start.1 = (bf16[5,8,1,512]{3,2,1,0:T(2,128)(2,1)S(1)}, bf16[5,8,1,512]{3,2,1,0:T(2,128)(2,1)}, u32[]{:S(2)}, u32[]{:S(2)}) collective-permute-start(bf16[5,8,1,512]{3,2,1,0:T(2,128)(2,1)S(1)} %get-tuple-element.59), channel_id=1, source_target_pairs={{1,0},{2,1},{3,2},{4,3},{5,4},{6,5},{7,6},{8,7},{9,8},{10,9},{11,1... | collective-permute-start | bytes 122888 | tf_op jit(solution)/shard_map/ppermute | solution.py:34
  354.6 4.0 copy-start.10
  362.7 18.8 %all-to-all-start.1 = ((bf16[32,2,2,4]{3,1,2,0:T(2,128)(2,1)}), bf16[32,2,2,4]{3,1,2,0:T(2,128)(2,1)S(1)}, u32[]{:S(2)}, u32[]{:S(2)}) async-start(bf16[32,2,2,4]{3,1,2,0:T(2,128)(2,1)} %copy.43), calls=%async_computation.1 | async-start | bytes 65536 | tf_op jit(solution)/shard_map/all_to_all | solution.py:138
  371.0 10.6 %copy-start.24 = (s32[48]{0:T(128)S(1)}, s32[48]{0:T(128)}, u32[]{:S(2)}) copy-start(s32[48]{0:T(128)} %copy-done.23) | copy-start | bytes 580
  371.0 11.1 %copy-start.19 = (s32[192,1]{0,1:T(1,128)S(1)}, s32[192,1]{0,1:T(1,128)}, u32[]{:S(2)}) copy-start(s32[192,1]{0,1:T(1,128)} %get-tuple-element.72) | copy-start | bytes 2308
  402.3 241.9 %copy-start.1 = (bf16[12,2048]{1,0:T(8,128)(2,1)S(1)}, bf16[12,2048]{1,0:T(8,128)(2,1)}, u32[]{:S(2)}) copy-start(bf16[12,2048]{1,0:T(8,128)(2,1)} %param.19) | copy-start | bytes 147460
Sparse Core Ops, SparseCore 0:
  10.8 159.3 all-gather.1
  332.7 120.1 all-reduce.1
  455.7 186.8 reduce-scatter.1
